TPU v7x, 128 devices: a whole 4x4x4 slice. The times are simulated.
128 devices in a mesh: prow: 8 (over y_lo, z), pcol: 16 (over x, y_hi, core).
Axes of the slice: x: 4, y: 4 (y_hi: 2, y_lo: 2; y = y_hi * 2 + y_lo), z: 4, core: 2. Of those that a mesh axis runs over, the one named last changes fastest.
Arguments:
- anc_inverse: float32 [4096, 4096], P('pcol', 'prow')
- pattern_one: int32 [16, 8], replicated, may hold values from 0 to 15, as said below
- parents: int32 [16], replicated, may hold values from 0 to 15, as said below
- low_one: float32 [16, 2048, 256], P('pcol', 'prow'), may hold values from -2 to 2
- pivot_one: float32 [16, 256, 256], P('pcol'), may hold values from -4 to 4
- low_two: float32 [16, 2048, 256], P('pcol', 'prow'), may hold values from -2 to 2
- second_scaled_factor: float32 [16, 256, 256], P('pcol'), may hold values from -2 to 2
- second_pivot_inverse: float32 [16, 256, 256], P('pcol'), may hold values from -4 to 4
Outputs:
- column_one: float32 [16, 4096, 256], P('prow', 'pcol')
- diag_one: float32 [16, 256, 256], P('pcol')
- column_two: float32 [16, 4096, 256], P('prow', 'pcol')
- second_parent_inverse: float32 [16, 256, 256], P('pcol')
- second_diagonal_inverse: float32 [16, 256, 256], P('pcol')
Inputs may be any that keep to these rules, and one draw needn't show every extreme that they name: `pattern_one`: entry r of each row names an ancestor of process row r: it lies in r * 2 to r * 2 + 1; for each r, every ancestor of that range is entry r of exactly 8 rows. `parents`: every first-level supernode is the parent of exactly one second-level supernode.
All inputs are finite; a program needn't handle non-finite values.
Results may differ from a plain program's by a relative error of at most 0.000073.
Values sent between devices are 32-bit elements; how exact they have to be, the bound alone decides.
No kernel may reach another device: no remote copies, remote signals or barrier semaphores. Data moves between devices by JAX's collectives and lax.ppermute only.
A program may use at most 128 MiB of HBM per device.

v0:
```python
import jax
import jax.numpy as jnp
from jax import lax
from jax.sharding import PartitionSpec as P


def in_one_piece(arrays, axis, dim, along):
    widths = [a.shape[along] for a in arrays]
    both = jnp.concatenate(arrays, axis=along)
    result = lax.all_gather(both, axis, axis=dim, tiled=True)
    return tuple(jnp.split(result, [sum(widths[:k]) for k in range(1, len(widths))], axis=along))


def sent_to_all(x, axis):
    copies = jnp.broadcast_to(x, (lax.axis_size(axis), *x.shape))
    return lax.all_to_all(copies, axis, split_axis=0, concat_axis=0, tiled=True)


def over_copies(x, axis):
    return sent_to_all(x, axis).sum(axis=0)


def side_by_side(arrays, axis, dim, along):
    both = jnp.concatenate(arrays, axis=along)
    result, at, outs = (lax.psum_scatter(both, axis, scatter_dimension=dim, tiled=True), 0, [])
    for a in arrays:
        outs.append(lax.slice_in_dim(result, at, at + a.shape[along], axis=along))
        at += a.shape[along]
    return tuple(outs)


def together(arrays, axis):
    line, at, outs = (jnp.concatenate([a.reshape(-1) for a in arrays]), 0, [])
    subtotal = over_copies(line, axis)
    for a in arrays:
        outs.append(subtotal[at : at + a.size].reshape(a.shape))
        at += a.size
    return tuple(outs)


def batched(left, right):
    return jnp.einsum("kab,kbd->kad", left, right, precision=lax.Precision.HIGHEST)


def batched_left_t(left, right):
    return jnp.einsum("kba,kbd->kad", left, right, precision=lax.Precision.HIGHEST)


def pick_rows(hit_mask, count):
    total = hit_mask.shape[0]
    keys = jnp.where(hit_mask, 0, total).astype(jnp.int32) + jnp.arange(total, dtype=jnp.int32)
    chosen_rows = jnp.argsort(keys)[:count]
    valid = jnp.take(hit_mask, chosen_rows, axis=0).astype(jnp.float32)[:, None, None]
    return (chosen_rows, valid)


def body(
    anc_inverse,
    pattern_one,
    parents,
    low_one,
    pivot_one,
    low_two,
    second_scaled_factor,
    second_pivot_inverse,
):
    my_row = lax.axis_index("prow")
    my_col = lax.axis_index("pcol")
    row_count = lax.axis_size("prow")
    col_count = lax.axis_size("pcol")
    per_row_anc = col_count // row_count
    supernode_block_width = pivot_one.shape[1]
    per_col_one = pivot_one.shape[0]
    per_col_two = second_scaled_factor.shape[0]
    owned = anc_inverse.shape[1] // supernode_block_width
    zblocks = anc_inverse.reshape(supernode_block_width, owned, supernode_block_width).transpose(
        1, 0, 2
    )
    lowall = lax.all_gather(low_one, "pcol", axis=0, tiled=True)
    total_one = lowall.shape[0]
    owned_slot_list = lax.dynamic_index_in_dim(pattern_one, my_row, 1, keepdims=False)
    chosen = jnp.take(zblocks, owned_slot_list - my_row * owned, axis=0)
    first_terms = batched(chosen, lowall)
    lowsec, topall = in_one_piece((low_two, second_scaled_factor), "pcol", 0, 1)
    total_two = lowsec.shape[0]
    pattern_two = jnp.take(pattern_one, parents, axis=0)
    my_slots_two = lax.dynamic_index_in_dim(pattern_two, my_row, 1, keepdims=False)
    chosen_two = jnp.take(zblocks, my_slots_two - my_row * owned, axis=0)
    first_full = -lax.psum(first_terms, "prow")
    share = total_two // row_count
    start = my_row * share
    parents_share = lax.dynamic_slice_in_dim(parents, start, share, 0)
    tops_share = lax.dynamic_slice_in_dim(topall, start, share, 0)
    carried = batched(jnp.take(first_full, parents_share, axis=0), tops_share)
    base_terms = batched(chosen_two, lowsec)
    updated = lax.dynamic_slice_in_dim(base_terms, start, share, 0) + carried
    second_terms = lax.dynamic_update_slice_in_dim(base_terms, updated, start, 0)
    second_full = -lax.psum(second_terms, "prow")
    rows_one, valid_one = pick_rows(owned_slot_list == my_col, total_one // per_row_anc)
    pivot_small = valid_one * batched_left_t(
        jnp.take(lowall, rows_one, axis=0), jnp.take(first_full, rows_one, axis=0)
    )
    pivot_terms = jnp.zeros_like(first_full).at[rows_one].add(pivot_small)
    pivot_part = lax.psum_scatter(pivot_terms, "pcol", scatter_dimension=0, tiled=True)
    pivot_sum = over_copies(pivot_part, "prow")
    diag_one = pivot_one - pivot_sum
    count_one = first_full.shape[0] // row_count
    column_one = lax.dynamic_slice_in_dim(first_full, my_row * count_one, count_one, 0)
    second_level_count = second_full.shape[0] // row_count
    column_two = lax.dynamic_slice_in_dim(
        second_full, my_row * second_level_count, second_level_count, 0
    )
    rows_two, valid_two = pick_rows(my_slots_two == my_col, total_two // per_row_anc)
    lows_picked = jnp.take(lowsec, rows_two, axis=0)
    parent_picked = jnp.take(first_full, jnp.take(parents, rows_two, axis=0), axis=0)
    cross_small = valid_two * batched_left_t(parent_picked, lows_picked)
    diag_small = valid_two * batched_left_t(lows_picked, jnp.take(second_full, rows_two, axis=0))
    local_parent = parents - my_col * per_col_one
    own_parent = (local_parent >= 0) & (local_parent < per_col_one)
    rows_own, valid_own = pick_rows(own_parent, per_col_two)
    valid_own = valid_own * (my_row == 0).astype(jnp.float32)
    local_picked = jnp.clip(jnp.take(local_parent, rows_own, axis=0), 0, per_col_one - 1)
    picked = jnp.take(diag_one, local_picked, axis=0)
    own_small = valid_own * batched(picked, jnp.take(topall, rows_own, axis=0))
    cross_terms = (
        jnp.zeros_like(second_full).at[rows_two].add(cross_small).at[rows_own].add(own_small)
    )
    diag_terms = jnp.zeros_like(second_full).at[rows_two].add(diag_small)
    part_cross, part_diag = side_by_side((cross_terms, diag_terms), "pcol", 0, 1)
    sum_cross, sum_diag = together((part_cross, part_diag), "prow")
    second_parent_inverse = -sum_cross
    second_diagonal_inverse = (
        second_pivot_inverse
        - batched_left_t(second_scaled_factor, second_parent_inverse)
        - sum_diag
    )
    return (column_one, diag_one, column_two, second_parent_inverse, second_diagonal_inverse)


def solution(mesh):
    placed = (
        P("pcol", "prow"),
        P(),
        P(),
        P("pcol", "prow", None),
        P("pcol", None, None),
        P("pcol", "prow", None),
        P("pcol", None, None),
        P("pcol", None, None),
    )
    return jax.shard_map(
        body,
        mesh=mesh,
        in_specs=placed,
        out_specs=(
            P("prow", "pcol", None),
            P("pcol", None, None),
            P("prow", "pcol", None),
            P("pcol", None, None),
            P("pcol", None, None),
        ),
        check_vma=False,
    )
```

profile of v0, /device:TPU:1, one launch (start us, length us, event | category | flops | bytes accessed | tf_op | source)
XLA Modules:
  0.0 673.7 jit_solution(4868192869001686954)
XLA Ops:
  7.9 1.2 copy.59
  11.0 2.8 gather_fusion.3
  13.8 56.2 %all-gather.3.cloned.1.call-done = f32[16,256,256]{2,1,0:T(8,128)} async-done(((f32[1,256,256]{2,1,0:T(8,128)}), f32[16,256,256]{2,1,0:T(8,128)}) %all-gather.3.cloned.1.call-update) | async-done | bytes 4194320 | tf_op jit(solution)/shard_map/all_gather | solution.py:79
  70.0 9.7 %fusion.2 = f32[16,256,256]{2,1,0:T(8,128)} fusion(f32[16,256,256]{2,1,0:T(8,128)} %all-gather.3.cloned.1.call-done, f32[16,256,256]{2,1,0:T(8,128)} %gather_fusion.3, pred[16]{0:T(512)(128)(4,1)S(1)} %compare_and_fusion.4), kind=kOutput, calls=%fused_computation.18 | convolution fusion | flops 3222274048 | bytes 12582928 | tf_op jit(solution)/shard_map/kab,kbd->kad/dot_general | solution.py:42
  79.8 0.9 copy-done.6
  81.9 1.2 sort.45
  83.8 4.2 gather_fusion.5
  88.0 95.9 %all-reduce.3.cloned.1.call-done = f32[16,256,256]{2,1,0:T(8,128)} async-done(((f32[16,256,256]{2,1,0:T(8,128)}), f32[16,256,256]{2,1,0:T(8,128)}) %all-reduce.3.cloned.1.call-update) | async-done | bytes 4194320 | tf_op jit(solution)/shard_map/psum | solution.py:89
  183.9 4.5 neg.15
  188.4 4.2 gather_fusion.6
  192.6 6.1 fusion.17
  198.7 2.4 broadcast.189.clone
  201.1 4.4 scatter_fusion
  207.0 2.7 gather_fusion.7
  209.8 2.8 gather_fusion.1
  212.6 46.1 %all-gather.5.cloned.1.call-done = f32[16,512,256]{2,1,0:T(8,128)} async-done(((f32[1,512,256]{2,1,0:T(8,128)}), f32[16,512,256]{2,1,0:T(8,128)}) %all-gather.5.cloned.1.call-update) | async-done | bytes 8388624 | tf_op jit(solution)/shard_map/all_gather | solution.py:10
  258.7 6.4 fusion.67
  265.9 1.3 copy-done.2
  267.2 5.6 fusion
  272.9 2.5 fusion.32
  275.4 63.5 %reduce-scatter.3.cloned.1.call-done = f32[1,256,256]{2,1,0:T(8,128)} async-done(((f32[16,256,256]{2,1,0:T(8,128)}), f32[1,256,256]{2,1,0:T(8,128)}) %reduce-scatter.3.cloned.1.call-update) | async-done | bytes 262160 | tf_op jit(solution)/shard_map/reduce_scatter | solution.py:104
  339.0 2.5 broadcast_in_dim.110
  341.5 4.4 all-to-all-start
  345.9 1.2 sort.46
  348.5 1.2 sort.47
  353.0 4.2 gather_fusion.9
  357.2 2.9 gather_fusion.10
  360.1 6.7 %fusion.22 = f32[8,256,256]{2,1,0:T(8,128)} fusion(f32[8,256,256]{2,1,0:T(8,128)S(1)} %gather_fusion.10, f32[8,256,256]{2,1,0:T(8,128)} %gather_fusion.9, f32[8]{0:T(128)S(1)} %get-tuple-element.106, pred[8]{0:T(512)(128)(4,1)S(1)} %get-tuple-element.93, pred[8]{0:T(512)(128)(4,1)S(1)} %get-tuple-element.91), kind=kOutput, calls=%fused_computation.34 | convolution fusion | flops 1612185600 | bytes 6291504 | tf_op jit(solution)/shard_map/kba,kbd->kad/dot_general | solution.py:46
  366.9 2.4 broadcast.189.clone.2
  369.3 5.3 scatter_fusion.1
  374.6 90.7 %all-reduce.5.cloned.1.call-done = f32[16,256,256]{2,1,0:T(8,128)} async-done(((f32[16,256,256]{2,1,0:T(8,128)}), f32[16,256,256]{2,1,0:T(8,128)}) %all-reduce.5.cloned.1.call-update) | async-done | bytes 4194320 | tf_op jit(solution)/shard_map/psum | solution.py:98
  465.3 4.5 neg.16
  469.7 4.2 gather_fusion.11
  474.0 6.7 fusion.27
  480.7 2.4 broadcast.189.clone.1
  483.0 4.4 scatter_fusion.2
  487.4 1.8 reduce_sum.20
  489.2 2.8 fusion.36
  492.0 7.4 %pad_maximum_fusion = f32[16,512,256]{2,1,0:T(8,128)} fusion(f32[16,256,256]{2,1,0:T(8,128)} %scatter_fusion.2, f32[16,256,256]{2,1,0:T(8,128)} %fusion.36), kind=kLoop, calls=%fused_computation.15 | loop fusion | flops 2097152 | bytes 16777216 | tf_op jit(solution)/shard_map/concatenate | solution.py:24
  499.5 100.2 %reduce-scatter.5.cloned.1.call-done = f32[1,512,256]{2,1,0:T(8,128)} async-done(((f32[16,512,256]{2,1,0:T(8,128)}), f32[1,512,256]{2,1,0:T(8,128)}) %reduce-scatter.5.cloned.1.call-update) | async-done | bytes 524304 | tf_op jit(solution)/shard_map/reduce_scatter | solution.py:25
  599.7 1.1 slice_bitcast_fusion.1
  601.1 4.1 broadcast_in_dim.125
  605.2 4.9 all-to-all-start.1
  610.3 1.9 constant_dynamic-slice_fusion.1
  612.1 1.9 constant_dynamic-slice_fusion
  614.0 44.8 %all-to-all-done.1 = f32[8,1,131072]{2,1,0:T(1,128)} async-done(((f32[8,1,131072]{2,1,0:T(1,128)}), f32[8,1,131072]{2,1,0:T(1,128)}, u32[]{:S(2)}, u32[]{:S(2)}) %all-to-all-start.1) | async-done | bytes 4194336 | tf_op jit(solution)/shard_map/all_to_all | solution.py:16
  658.8 5.2 reduce_sum.22
  665.7 0.8 copy.68
  (80 shorter events, 12.4 us)
Async XLA Ops:
  7.2 62.9 %all-gather.3.cloned.1.call-start = ((), (), s32[]{:S(2)}) async-start(), calls=%async_computation.4 | async-start | bytes 4456448 | tf_op jit(solution)/shard_map/all_gather | solution.py:79
  7.9 176.0 %all-reduce.3.cloned.1.call-start = ((), (), s32[]{:S(2)}) async-start(), calls=%async_computation.5 | async-start | bytes 8388608 | tf_op jit(solution)/shard_map/psum | solution.py:89
  79.7 0.9 copy-start.6
  79.7 1.0 copy-start.9
  79.8 178.9 %all-gather.5.cloned.1.call-start = ((), (), s32[]{:S(2)}) async-start(), calls=%async_computation.7 | async-start | bytes 8912896 | tf_op jit(solution)/shard_map/all_gather | solution.py:10
  81.6 257.4 %reduce-scatter.3.cloned.1.call-start = ((), (), s32[]{:S(2)}) async-start(), calls=%async_computation.6 | async-start | bytes 4456448 | tf_op jit(solution)/shard_map/reduce_scatter | solution.py:104
  201.1 4.9 copy-start
  205.5 259.8 %all-reduce.5.cloned.1.call-start = ((), (), s32[]{:S(2)}) async-start(), calls=%async_computation.8 | async-start | bytes 8388608 | tf_op jit(solution)/shard_map/psum | solution.py:98
  258.7 7.2 %copy-start.1 = (f32[16,512,256]{2,1,0:T(8,128)S(1)}, f32[16,512,256]{2,1,0:T(8,128)}, u32[]{:S(2)}) copy-start(f32[16,512,256]{2,1,0:T(8,128)} %all-gather.5.cloned.1.call-done) | copy-start | bytes 25165828
  258.7 8.5 %copy-start.2 = (f32[16,256,256]{2,1,0:T(8,128)S(1)}, f32[16,256,256]{2,1,0:T(8,128)}, u32[]{:S(2)}) copy-start(f32[16,256,256]{2,1,0:T(8,128)} %gather_fusion.7) | copy-start | bytes 12582916
  267.2 5.6 copy-start.4
  275.4 76.9 %copy-start.10 = (s32[3]{0:T(128)S(1)}, s32[3]{0:T(128)}, u32[]{:S(2)}) copy-start(s32[3]{0:T(128)} %constant.173.clone.1) | copy-start | bytes 40
  341.5 145.9 %all-to-all-start = ((f32[8,1,256,256]{3,2,1,0:T(8,128)}), f32[8,1,256,256]{3,2,1,0:T(8,128)}, u32[]{:S(2)}, u32[]{:S(2)}) async-start(f32[8,1,256,256]{3,2,1,0:T(8,128)} %broadcast_in_dim.110), calls=%async_computation.1 | async-start | bytes 4194304 | tf_op jit(solution)/shard_map/all_to_all | solution.py:16
  345.9 253.8 %reduce-scatter.5.cloned.1.call-start = ((), (), s32[]{:S(2)}) async-start(), calls=%async_computation.9 | async-start | bytes 8912896 | tf_op jit(solution)/shard_map/reduce_scatter | solution.py:25
  480.7 2.4 copy-start.3
  483.0 6.1 copy-start.7
  489.2 10.2 %copy-start.5 = (f32[1,256,256]{2,1,0:T(8,128)}, f32[1,256,256]{2,1,0:T(8,128)S(1)}, u32[]{:S(2)}) copy-start(f32[1,256,256]{2,1,0:T(8,128)S(1)} %bitcast_subtract_fusion) | copy-start | bytes 786436
  605.2 4.9 copy-start.8
  605.2 53.5 %all-to-all-start.1 = ((f32[8,1,131072]{2,1,0:T(1,128)}), f32[8,1,131072]{2,1,0:T(1,128)}, u32[]{:S(2)}, u32[]{:S(2)}) async-start(f32[8,1,131072]{2,1,0:T(1,128)} %broadcast_in_dim.125), calls=%async_computation.3 | async-start | bytes 8388608 | tf_op jit(solution)/shard_map/all_to_all | solution.py:16
Sparse Core Ops, SparseCore 0:
  10.4 59.5 all-gather.2
  79.9 103.9 all-reduce.2
  186.9 71.8 all-gather.4
  262.6 76.3 reduce-scatter.2
  341.5 123.7 all-reduce.4
  499.6 100.0 reduce-scatter.4
where the time goes:
time: 683 us; the launch traced here: 674 us
  waiting for transfers between devices  498 us (73%)
  local copies, waits for them, and re-layouts  64.3 us (9%)
  other arithmetic  44.5 us (7%)
  matrix products  40.7 us (6%)
  between operations  16 us (2%)
  starting transfers between devices  9.97 us (1%)
    reduce_scatter x1, waiting for transfers between devices, side_by_side(): lax.psum_scatter(both, axis, scatter_dimension=dim, tiled=True)  100 us
    psum x1, waiting for transfers between devices, body(): first_full = -lax.psum(first_terms, 'prow')  95.9 us
    psum x1, waiting for transfers between devices, body(): second_full = -lax.psum(second_terms, 'prow')  90.7 us
    reduce_scatter x1, waiting for transfers between devices, body(): lax.psum_scatter(pivot_terms, 'pcol', scatter_dimension=0, tiled=True)  63.5 us
    all_gather x1, waiting for transfers between devices, body(): lowall = lax.all_gather(low_one, 'pcol', axis=0, tiled=True)  56.2 us
    all_gather x1, waiting for transfers between devices, in_one_piece(): result = lax.all_gather(both, axis, axis=dim, tiled=True)  46.1 us
    all_to_all x2, waiting for transfers between devices, sent_to_all(): return lax.all_to_all(copies, axis, split_axis=0, concat_axis=0, tiled=True)  44.8 us
    dot_general x4, matrix products, batched(): jnp.einsum('kab,kbd->kad', left, right, precision=lax.Precision.HIGHEST)  20.6 us
  transfers between devices with their start and end apart: 8, of which 7 were waited for; matrix products, arithmetic and copies ran while one was open for 17% of the time, Pallas kernels for 0%

commit v1 on v0

--- a/solution.py
+++ b/solution.py
@@ -95,7 +95,7 @@
     base_terms = batched(chosen_two, lowsec)
     updated = lax.dynamic_slice_in_dim(base_terms, start, share, 0) + carried
     second_terms = lax.dynamic_update_slice_in_dim(base_terms, updated, start, 0)
-    second_full = -lax.psum(second_terms, "prow")
+    second_full = -jnp.sum(lax.all_gather(second_terms, "prow"), axis=0)
     rows_one, valid_one = pick_rows(owned_slot_list == my_col, total_one // per_row_anc)
     pivot_small = valid_one * batched_left_t(
         jnp.take(lowall, rows_one, axis=0), jnp.take(first_full, rows_one, axis=0)

time: 683 us -> 916 us (1.34)
  waiting for transfers between devices: 498 us -> 713 us
  other arithmetic: 44.5 us -> 58.8 us
    all_gather x0 -> x1, waiting for transfers between devices: none -> 294 us  [body(): second_full = -jnp.sum(lax.all_gather(second_terms, 'prow'), axis=0)]
    psum x1 -> x0, waiting for transfers between devices: 90.7 us -> none  [body(): second_full = -lax.psum(second_terms, 'prow')]
    all_to_all x2, waiting for transfers between devices: 44.8 us -> 60.1 us  [sent_to_all(): return lax.all_to_all(copies, axis, split_axis=0, concat_axis=0, tiled=True)]
    reduce_sum x0 -> x1, other arithmetic: none -> 14.3 us  [body(): second_full = -jnp.sum(lax.all_gather(second_terms, 'prow'), axis=0)]
  transfers between devices with their start and end apart: 8 -> 8, of which waited for: 7 -> 8; matrix products, arithmetic and copies ran while one was open for 17% -> 10% of each run, Pallas kernels for 0% -> 0%
where the time goes in v1:
time: 916 us; the launch traced here: 906 us
  waiting for transfers between devices  713 us (78%)
  local copies, waits for them, and re-layouts  65.8 us (7%)
  other arithmetic  58.8 us (6%)
  matrix products  42.4 us (5%)
  between operations  16 us (2%)
  starting transfers between devices  9.93 us (1%)
    all_gather x1, waiting for transfers between devices, body(): second_full = -jnp.sum(lax.all_gather(second_terms, 'prow'), axis=0)  294 us
    reduce_scatter x1, waiting for transfers between devices, side_by_side(): lax.psum_scatter(both, axis, scatter_dimension=dim, tiled=True)  99.5 us
    psum x1, waiting for transfers between devices, body(): first_full = -lax.psum(first_terms, 'prow')  95.9 us
    reduce_scatter x1, waiting for transfers between devices, body(): lax.psum_scatter(pivot_terms, 'pcol', scatter_dimension=0, tiled=True)  60.6 us
    all_to_all x2, waiting for transfers between devices, sent_to_all(): return lax.all_to_all(copies, axis, split_axis=0, concat_axis=0, tiled=True)  60.1 us
    all_gather x1, waiting for transfers between devices, body(): lowall = lax.all_gather(low_one, 'pcol', axis=0, tiled=True)  56.2 us
    all_gather x1, waiting for transfers between devices, in_one_piece(): result = lax.all_gather(both, axis, axis=dim, tiled=True)  45.9 us
    dot_general x4, matrix products, batched(): jnp.einsum('kab,kbd->kad', left, right, precision=lax.Precision.HIGHEST)  22.3 us
  transfers between devices with their start and end apart: 8, of which 8 were waited for; matrix products, arithmetic and copies ran while one was open for 10% of the time, Pallas kernels for 0%

profile of v1, /device:TPU:1, one launch (start us, length us, event | category | flops | bytes accessed | tf_op | source)
XLA Modules:
  0.0 906.3 jit_solution(16188759240108930172)
XLA Ops:
  11.0 2.8 gather_fusion.3
  13.8 56.2 %all-gather.4.cloned.1.call-done = f32[16,256,256]{2,1,0:T(8,128)} async-done(((f32[1,256,256]{2,1,0:T(8,128)}), f32[16,256,256]{2,1,0:T(8,128)}) %all-gather.4.cloned.1.call-update) | async-done | bytes 4194320 | tf_op jit(solution)/shard_map/all_gather | solution.py:79
  70.0 9.7 %fusion.2 = f32[16,256,256]{2,1,0:T(8,128)} fusion(f32[16,256,256]{2,1,0:T(8,128)} %all-gather.4.cloned.1.call-done, f32[16,256,256]{2,1,0:T(8,128)} %gather_fusion.3, pred[16]{0:T(512)(128)(4,1)S(1)} %compare_and_fusion.4), kind=kOutput, calls=%fused_computation.18 | convolution fusion | flops 3222274048 | bytes 12582928 | tf_op jit(solution)/shard_map/kab,kbd->kad/dot_general | solution.py:42
  81.9 1.2 sort.45
  83.8 4.2 gather_fusion.5
  88.0 95.9 %all-reduce.2.cloned.1.call-done = f32[16,256,256]{2,1,0:T(8,128)} async-done(((f32[16,256,256]{2,1,0:T(8,128)}), f32[16,256,256]{2,1,0:T(8,128)}) %all-reduce.2.cloned.1.call-update) | async-done | bytes 4194320 | tf_op jit(solution)/shard_map/psum | solution.py:89
  183.9 4.6 neg.15
  188.4 4.2 gather_fusion.6
  192.6 6.1 fusion.17
  198.7 2.5 broadcast.189.clone
  201.2 4.4 scatter_fusion
  207.2 2.8 gather_fusion.7
  210.0 2.8 gather_fusion.1
  212.8 45.9 %all-gather.6.cloned.1.call-done = f32[16,512,256]{2,1,0:T(8,128)} async-done(((f32[1,512,256]{2,1,0:T(8,128)}), f32[16,512,256]{2,1,0:T(8,128)}) %all-gather.6.cloned.1.call-update) | async-done | bytes 8388624 | tf_op jit(solution)/shard_map/all_gather | solution.py:10
  258.7 8.3 fusion
  267.1 2.2 copy.79
  269.2 3.1 copy-done.1
  272.3 2.6 fusion.68
  274.9 1.9 copy-done.3
  276.8 1.5 fusion.33
  278.3 60.6 %reduce-scatter.3.cloned.1.call-done = f32[1,256,256]{2,1,0:T(8,128)} async-done(((f32[16,256,256]{2,1,0:T(8,128)}), f32[1,256,256]{2,1,0:T(8,128)}) %reduce-scatter.3.cloned.1.call-update) | async-done | bytes 262160 | tf_op jit(solution)/shard_map/reduce_scatter | solution.py:104
  339.0 2.4 broadcast_in_dim.110
  341.4 4.3 all-to-all-start
  345.8 1.2 sort.46
  348.4 1.2 sort.47
  352.9 4.6 gather_fusion.9
  357.5 2.9 gather_fusion.10
  360.4 6.7 fusion.22
  367.1 2.3 broadcast.189.clone.2
  369.4 5.3 scatter_fusion.1
  374.7 15.3 %all-to-all-done = f32[8,1,256,256]{3,2,1,0:T(8,128)} async-done(((f32[8,1,256,256]{3,2,1,0:T(8,128)}), f32[8,1,256,256]{3,2,1,0:T(8,128)}, u32[]{:S(2)}, u32[]{:S(2)}) %all-to-all-start) | async-done | bytes 2097184 | tf_op jit(solution)/shard_map/all_to_all | solution.py:16
  390.0 1.8 reduce_sum.29
  391.8 2.8 fusion.37
  394.6 294.3 %all-gather.8.cloned.1.call-done = f32[8,16,256,256]{3,2,1,0:T(8,128)} async-done(((f32[1,16,256,256]{3,2,1,0:T(8,128)}), f32[8,16,256,256]{3,2,1,0:T(8,128)}) %all-gather.8.cloned.1.call-update) | async-done | bytes 33554448 | tf_op jit(solution)/shard_map/all_gather | solution.py:98
  688.9 14.3 %reduce_sum.31 = f32[16,256,256]{2,1,0:T(8,128)} reduce(f32[8,16,256,256]{3,2,1,0:T(8,128)} %all-gather.8.cloned.1.call-done, f32[]{:T(128)} %constant.166.clone.1), dimensions={0}, to_apply=%region_5.9 | reduce | flops 7340032 | bytes 37748740 | tf_op jit(solution)/shard_map/reduce_sum | solution.py:98
  703.2 4.5 neg.16
  707.7 4.2 gather_fusion.11
  711.8 6.7 fusion.27
  718.5 2.4 broadcast.189.clone.1
  721.0 4.4 scatter_fusion.2
  725.4 7.4 pad_maximum_fusion
  732.8 99.5 %reduce-scatter.5.cloned.1.call-done = f32[1,512,256]{2,1,0:T(8,128)} async-done(((f32[16,512,256]{2,1,0:T(8,128)}), f32[1,512,256]{2,1,0:T(8,128)}) %reduce-scatter.5.cloned.1.call-update) | async-done | bytes 524304 | tf_op jit(solution)/shard_map/reduce_scatter | solution.py:25
  833.7 4.1 broadcast_in_dim.125
  837.9 4.9 all-to-all-start.1
  842.9 1.9 constant_dynamic-slice_fusion.1
  844.8 1.9 constant_dynamic-slice_fusion
  846.6 44.8 %all-to-all-done.1 = f32[8,1,131072]{2,1,0:T(1,128)} async-done(((f32[8,1,131072]{2,1,0:T(1,128)}), f32[8,1,131072]{2,1,0:T(1,128)}, u32[]{:S(2)}, u32[]{:S(2)}) %all-to-all-start.1) | async-done | bytes 4194336 | tf_op jit(solution)/shard_map/all_to_all | solution.py:16
  891.4 5.2 reduce_sum.32
  (80 shorter events, 15.5 us)
Async XLA Ops:
  7.2 62.9 %all-gather.4.cloned.1.call-start = ((), (), s32[]{:S(2)}) async-start(), calls=%async_computation.4 | async-start | bytes 4456448 | tf_op jit(solution)/shard_map/all_gather | solution.py:79
  7.9 176.0 %all-reduce.2.cloned.1.call-start = ((), (), s32[]{:S(2)}) async-start(), calls=%async_computation.5 | async-start | bytes 8388608 | tf_op jit(solution)/shard_map/psum | solution.py:89
  79.7 0.9 copy-start.5
  79.7 1.0 copy-start.8
  79.8 178.9 %all-gather.6.cloned.1.call-start = ((), (), s32[]{:S(2)}) async-start(), calls=%async_computation.7 | async-start | bytes 8912896 | tf_op jit(solution)/shard_map/all_gather | solution.py:10
  81.6 257.4 %reduce-scatter.3.cloned.1.call-start = ((), (), s32[]{:S(2)}) async-start(), calls=%async_computation.6 | async-start | bytes 4456448 | tf_op jit(solution)/shard_map/reduce_scatter | solution.py:104
  201.2 5.0 copy-start
  205.6 483.3 %all-gather.8.cloned.1.call-start = ((), (), s32[]{:S(2)}) async-start(), calls=%async_computation.8 | async-start | bytes 37748736 | tf_op jit(solution)/shard_map/all_gather | solution.py:98
  267.0 5.3 copy-start.1
  274.9 1.9 copy-start.3
  278.3 73.9 %copy-start.9 = (s32[3]{0:T(128)S(1)}, s32[3]{0:T(128)}, u32[]{:S(2)}) copy-start(s32[3]{0:T(128)} %constant.174.clone.1) | copy-start | bytes 40
  341.4 48.6 %all-to-all-start = ((f32[8,1,256,256]{3,2,1,0:T(8,128)}), f32[8,1,256,256]{3,2,1,0:T(8,128)}, u32[]{:S(2)}, u32[]{:S(2)}) async-start(f32[8,1,256,256]{3,2,1,0:T(8,128)} %broadcast_in_dim.110), calls=%async_computation.1 | async-start | bytes 4194304 | tf_op jit(solution)/shard_map/all_to_all | solution.py:16
  345.8 486.6 %reduce-scatter.5.cloned.1.call-start = ((), (), s32[]{:S(2)}) async-start(), calls=%async_computation.9 | async-start | bytes 8912896 | tf_op jit(solution)/shard_map/reduce_scatter | solution.py:25
  369.4 22.3 %copy-start.6 = (f32[1,256,256]{2,1,0:T(8,128)S(1)}, f32[1,256,256]{2,1,0:T(8,128)}, u32[]{:S(2)}) copy-start(f32[1,256,256]{2,1,0:T(8,128)} %param.20) | copy-start | bytes 786436
  391.8 311.4 %copy-start.4 = (f32[1,256,256]{2,1,0:T(8,128)}, f32[1,256,256]{2,1,0:T(8,128)S(1)}, u32[]{:S(2)}) copy-start(f32[1,256,256]{2,1,0:T(8,128)S(1)} %bitcast_subtract_fusion) | copy-start | bytes 786436
  718.5 2.4 copy-start.2
  837.9 4.9 copy-start.7
  837.9 53.6 %all-to-all-start.1 = ((f32[8,1,131072]{2,1,0:T(1,128)}), f32[8,1,131072]{2,1,0:T(1,128)}, u32[]{:S(2)}, u32[]{:S(2)}) async-start(f32[8,1,131072]{2,1,0:T(1,128)} %broadcast_in_dim.125), calls=%async_computation.3 | async-start | bytes 8388608 | tf_op jit(solution)/shard_map/all_to_all | solution.py:16
Sparse Core Ops, SparseCore 0:
  10.4 59.5 all-gather.3
  79.9 103.9 all-reduce.1
  186.9 71.8 all-gather.5
  262.6 76.3 reduce-scatter.2
  340.6 348.3 all-gather.7
  732.9 99.3 reduce-scatter.4
